TPU v7x, 512 devices: a whole 4x4x16 slice. The times are simulated.
512 devices in a mesh: tube: 32 (over z, y_lo), gy: 4 (over y_hi, core), gz: 4 (over x).
Axes of the slice: x: 4, y: 4 (y_hi: 2, y_lo: 2; y = y_hi * 2 + y_lo), z: 16, core: 2. Of those that a mesh axis runs over, the one named last changes fastest.
Arguments:
- state: float32 [13, 512, 32, 512], P(None, 'tube', 'gy', 'gz'), as said below
- fresh: float32 [13, 32, 512], P(None, 'gy', 'gz'), as said below
- substeps: int32 [512, 32, 512], P('tube', 'gy', 'gz'), may hold values from 1 to 8, as said below
- shift: int32 [], replicated, may hold values from 1 to 12
Outputs:
- advanced: float32 [13, 512, 32, 512], P(None, 'tube', 'gy', 'gz')
Inputs may be any that keep to these rules, and one draw needn't show every extreme that they name: `state`: the first nine components are positive partial densities; the energy exceeds the kinetic and chemical energy by a positive thermal part. `fresh`: the same conventions as state. `substeps`: at most 8; some cell takes 8 in every draw.
All inputs are finite; a program needn't handle non-finite values.
Results may differ from a plain program's by a relative error of at most 0.0003.
Values sent between devices are 32-bit elements; how exact they have to be, the bound alone decides.
A program may use at most 64 MiB of HBM per device.

v0:
```python
import jax
import jax.numpy as jnp
import numpy as np
from jax import lax
from jax.sharding import PartitionSpec as P

SMAX = 12


molar_mass = (
    np.array([2.016, 31.998, 18.015, 1.008, 15.999, 17.007, 33.006, 34.014, 28.014]) / 18.015
)
heat_factor = np.array([2.5, 2.5, 3.0, 1.5, 1.5, 2.5, 3.0, 3.0, 2.5])
formation = np.array([0.0, 0.0, -1.5, 12.0, 1.5, 0.25, 0.02, -0.45, 0.0])
consumed_stoichiometry = [
    (3, 1, 9),
    (4, 5, 9),
    (4, 0, 9),
    (3, 5, 9),
    (0, 5, 9),
    (2, 3, 9),
    (4, 2, 9),
    (5, 5, 9),
    (0, 8, 9),
    (3, 3, 8),
    (4, 4, 8),
    (3, 4, 8),
    (3, 5, 8),
    (3, 1, 8),
    (6, 3, 9),
    (6, 3, 9),
    (6, 4, 9),
    (6, 5, 9),
    (6, 6, 9),
    (7, 8, 9),
    (7, 3, 9),
]
products = [
    (4, 5),
    (3, 1),
    (3, 5),
    (4, 0),
    (2, 3),
    (0, 5),
    (5, 5),
    (4, 2),
    (3, 3),
    (0,),
    (1,),
    (5,),
    (2,),
    (6,),
    (0, 1),
    (5, 5),
    (1, 5),
    (2, 1),
    (7, 1),
    (5, 5),
    (2, 5),
]
arrhenius_coefficients = [
    30.0,
    8.0,
    20.0,
    6.0,
    25.0,
    10.0,
    12.0,
    5.0,
    4.0,
    20.0,
    15.0,
    18.0,
    22.0,
    25.0,
    30.0,
    25.0,
    20.0,
    30.0,
    10.0,
    6.0,
    15.0,
]
arrhenius_barrier = [
    4.0,
    1.0,
    3.0,
    1.5,
    1.5,
    4.5,
    4.0,
    1.5,
    6.0,
    0.5,
    0.5,
    0.5,
    0.5,
    0.3,
    0.8,
    0.5,
    0.3,
    0.3,
    0.5,
    5.0,
    1.5,
]
time_step = 0.05


def from_behind(value, axis, steps):
    count = lax.axis_size(axis)
    first, last = (max(0, -steps), min(count, count - steps))
    return lax.ppermute(value, axis, [(source, source + steps) for source in range(first, last)])


def padded(cells, sides, width):
    for axis, dim in sides:
        count = lax.axis_size(axis)
        ends = count - 1
        head = lax.slice_in_dim(cells, 0, width, axis=dim)
        tail = lax.slice_in_dim(cells, cells.shape[dim] - width, cells.shape[dim], axis=dim)
        cells = jnp.concatenate(
            [
                lax.ppermute(tail, axis, [(i, (i + 1) % count) for i in range(ends)]),
                cells,
                lax.ppermute(head, axis, [((i + 1) % count, i) for i in range(ends)]),
            ],
            axis=dim,
        )
    return cells


def padded_2(x, sides, width):
    edges = {}
    for axis, dim in sides:
        devices, length = (lax.axis_size(axis), x.shape[dim])
        up = [(i, (i + 1) % devices) for i in range(devices)]
        last = lax.slice_in_dim(x, length - width, length, axis=dim)
        first = lax.slice_in_dim(x, 0, width, axis=dim)
        edges[dim] = (
            lax.ppermute(last, axis, up),
            lax.ppermute(first, axis, [(b, a) for a, b in up]),
        )
    done = []
    for _, dim in sides:
        low, high = edges[dim]
        around = [(width, width) if d in done else (0, 0) for d in range(x.ndim)]
        x = jnp.concatenate([jnp.pad(low, around), x, jnp.pad(high, around)], axis=dim)
        done.append(dim)
    return x


def stoich_table():
    table = np.zeros((9, 21))
    for constituent_count in range(21):
        for which in consumed_stoichiometry[constituent_count]:
            if which < 9:
                table[which, constituent_count] -= 1.0
        for which in products[constituent_count]:
            table[which, constituent_count] += 1.0
    return table * molar_mass[:, None]


def column(values, array):
    return jnp.asarray(values, dtype=array.dtype).reshape((9,) + (1,) * (array.ndim - 1))


def weno_side(first, second, third, fourth, fifth):
    smooth_a = (
        13.0 / 12.0 * (first - 2.0 * second + third) ** 2
        + 0.25 * (first - 4.0 * second + 3.0 * third) ** 2
    )
    smooth_b = 13.0 / 12.0 * (second - 2.0 * third + fourth) ** 2 + 0.25 * (second - fourth) ** 2
    smooth_c = (
        13.0 / 12.0 * (third - 2.0 * fourth + fifth) ** 2
        + 0.25 * (3.0 * third - 4.0 * fourth + fifth) ** 2
    )
    weight_a = 0.1 / (1e-06 + smooth_a) ** 2
    weight_b = 0.6 / (1e-06 + smooth_b) ** 2
    weight_c = 0.3 / (1e-06 + smooth_c) ** 2
    total = weight_a + weight_b + weight_c
    blend = (
        weight_a * (2.0 * first - 7.0 * second + 11.0 * third)
        + weight_b * (-second + 5.0 * third + 2.0 * fourth)
        + weight_c * (2.0 * third + 5.0 * fourth - fifth)
    )
    return blend / (6.0 * total)


def flux_change(ghosted_grid_values, array_axis, count):
    constituent_grids = ghosted_grid_values[:9]
    kilograms_per_volume = jnp.sum(constituent_grids, axis=0)
    momentum = ghosted_grid_values[9:12]
    motion_work = 0.5 * jnp.sum(momentum * momentum, axis=0) / kilograms_per_volume
    specific_warming_coefficient = jnp.sum(
        constituent_grids * column(heat_factor / molar_mass, constituent_grids), axis=0
    )
    combustion_portion = jnp.sum(constituent_grids * column(formation, constituent_grids), axis=0)
    kelvin_level = (
        ghosted_grid_values[12] - motion_work - combustion_portion
    ) / specific_warming_coefficient
    blend_accumulation = jnp.sum(
        constituent_grids * column(1.0 / molar_mass, constituent_grids), axis=0
    )
    thermodynamic_stress = blend_accumulation * kelvin_level
    sound = jnp.sqrt(
        (1.0 + blend_accumulation / specific_warming_coefficient)
        * thermodynamic_stress
        / kilograms_per_volume
    )
    row = 8 + array_axis
    fluid_speed_vector = ghosted_grid_values[row] / kilograms_per_volume
    flux = ghosted_grid_values * fluid_speed_vector[None]
    flux = jnp.concatenate(
        [
            flux[:row],
            (flux[row] + thermodynamic_stress)[None],
            flux[row + 1 : 12],
            (flux[12] + thermodynamic_stress * fluid_speed_vector)[None],
        ],
        axis=0,
    )
    speed = (jnp.abs(fluid_speed_vector) + sound)[None]

    def take(array, offset):
        return lax.slice_in_dim(array, offset, offset + count + 1, axis=array_axis)

    alpha = take(speed, 0)
    for offset in range(1, 6):
        alpha = jnp.maximum(alpha, take(speed, offset))
    plus = [
        0.5 * (take(flux, offset) + alpha * take(ghosted_grid_values, offset))
        for offset in range(5)
    ]
    minus = [
        0.5 * (take(flux, offset) - alpha * take(ghosted_grid_values, offset))
        for offset in range(1, 6)
    ]
    face = weno_side(plus[0], plus[1], plus[2], plus[3], plus[4]) + weno_side(
        minus[4], minus[3], minus[2], minus[1], minus[0]
    )
    return lax.slice_in_dim(face, 1, count + 1, axis=array_axis) - lax.slice_in_dim(
        face, 0, count, axis=array_axis
    )


def react_step(constituent_grids, thermal_content, step_size):
    specific_warming_coefficient = jnp.sum(
        constituent_grids * column(heat_factor / molar_mass, constituent_grids), axis=0
    )
    combustion_portion = jnp.sum(constituent_grids * column(formation, constituent_grids), axis=0)
    kelvin_level = (thermal_content - combustion_portion) / specific_warming_coefficient
    moles_per_volume = constituent_grids * column(1.0 / molar_mass, constituent_grids)
    moles_per_volume = jnp.concatenate(
        [moles_per_volume, jnp.ones_like(moles_per_volume[:1])], axis=0
    )
    progress_speeds = jnp.stack(
        [
            arrhenius_coefficients[constituent_count]
            * jnp.exp(-arrhenius_barrier[constituent_count] / kelvin_level)
            * moles_per_volume[consumed_stoichiometry[constituent_count][0]]
            * moles_per_volume[consumed_stoichiometry[constituent_count][1]]
            * moles_per_volume[consumed_stoichiometry[constituent_count][2]]
            for constituent_count in range(21)
        ]
    )
    table = jnp.asarray(stoich_table(), dtype=constituent_grids.dtype)
    omega = jnp.dot(table, progress_speeds, precision=lax.Precision.HIGHEST)
    return constituent_grids + step_size[None] * omega


def react_cells(constituent_grids, thermal_content, counts, turns):
    step_size = time_step / counts.astype(constituent_grids.dtype)

    def advance(index, current):
        moved = react_step(current, thermal_content, step_size)
        return jnp.where((index < counts)[None], moved, current)

    return lax.fori_loop(0, turns, advance, constituent_grids)


def react_blocks(constituent_grids, thermal_content, counts):
    cells = constituent_grids.shape[1]
    block = min(1024, cells)

    def one_block(constituent_count):
        lower = constituent_count * block
        part_species = lax.dynamic_slice_in_dim(constituent_grids, lower, block, 1)
        part_internal = lax.dynamic_slice_in_dim(thermal_content, lower, block, 0)
        part_counts = lax.dynamic_slice_in_dim(counts, lower, block, 0)
        return react_cells(part_species, part_internal, part_counts, jnp.max(part_counts))

    stacked = lax.map(one_block, jnp.arange(cells // block))
    return jnp.transpose(stacked, (1, 0, 2)).reshape(9, cells)


def repair(ghosted_grid_values, fresh, margin, rim):
    rows = ghosted_grid_values.shape[1]
    inner = rows - 2 * rim
    total = lax.axis_size("tube") * inner
    position = lax.axis_index("tube") * inner - rim + lax.iota(jnp.int32, rows)
    beyond = (position + margin >= total)[None, :, None, None]
    ghosted_grid_values = jnp.where(beyond, fresh[:, None], ghosted_grid_values)
    if rim > 0:
        before = (position < 0)[None, :, None, None]
        ghosted_grid_values = jnp.where(
            before, ghosted_grid_values[:, rim : rim + 1], ghosted_grid_values
        )
    return ghosted_grid_values


def on_device(state, fresh, substeps, shift):
    comps, planes, width_y, width_z = state.shape
    ahead = from_behind(state[:, :SMAX], "tube", -1)
    joined = jnp.concatenate([state, ahead], axis=1)
    start = repair(lax.dynamic_slice_in_dim(joined, shift, planes, 1), fresh, shift, 0)
    ghosted_grid_values = repair(padded(start, (("tube", 1),), 3), fresh, 0, 3)

    def evaluate(current, stream_ext):
        cross = padded_2(current, (("gy", 2), ("gz", 3)), 3)
        return -(
            flux_change(stream_ext, 1, planes)
            + flux_change(cross[:, :, :, 3 : width_z + 3], 2, width_y)
            + flux_change(cross[:, :, 3 : width_y + 3, :], 3, width_z)
        )

    def faces(current):
        return repair(padded(current, (("tube", 1),), 3), fresh, 0, 3)

    first = start + time_step * evaluate(start, ghosted_grid_values)
    second = 0.75 * start + 0.25 * (first + time_step * evaluate(first, faces(first)))
    third = 1.0 / 3.0 * start + 2.0 / 3.0 * (second + time_step * evaluate(second, faces(second)))
    kilograms_per_volume = jnp.sum(third[:9], axis=0)
    thermal_content = (
        third[12] - 0.5 * jnp.sum(third[9:12] * third[9:12], axis=0) / kilograms_per_volume
    )
    cells = planes * width_y * width_z
    constituent_grids = third[:9].reshape(9, cells)
    thermal_content = thermal_content.reshape(1, cells)
    counts = substeps.reshape(1, cells)
    reacted = react_blocks(constituent_grids, thermal_content[0], counts[0])
    return jnp.concatenate([reacted.reshape(9, planes, width_y, width_z), third[9:]], axis=0)


def solution(mesh):
    return jax.shard_map(
        on_device,
        mesh=mesh,
        in_specs=(P(None, "tube", "gy", "gz"), P(None, "gy", "gz"), P("tube", "gy", "gz"), P()),
        out_specs=P(None, "tube", "gy", "gz"),
        check_vma=False,
    )
```

profile of v0, /device:TPU:457, one launch (start us, length us, event | category | flops | bytes accessed | tf_op | source)
XLA Modules:
  0.0 441.1 jit_solution(13570674268264852574)
XLA Ops:
  4.2 15.1 %collective-permute-done = f32[13,12,8,128]{3,2,1,0:T(8,128)S(1)} collective-permute-done((f32[13,12,8,128]{3,2,1,0:T(8,128)S(1)}, f32[13,12,8,128]{3,2,1,0:T(8,128)S(1)}, u32[]{:S(2)}, u32[]{:S(2)}) %collective-permute-start) | collective-permute-done | bytes 639008 | tf_op jit(solution)/shard_map/ppermute | solution.py:113
  36.6 4.5 %collective-permute-start.4 = (f32[13,16,3,128]{3,1,2,0:T(8,128)}, f32[13,16,3,128]{3,1,2,0:T(8,128)S(1)}, u32[]{:S(2)}, u32[]{:S(2)}) collective-permute-start(f32[13,16,3,128]{3,1,2,0:T(8,128)} %get-tuple-element.358), channel_id=1, source_target_pairs={{4,0},{8,4},{12,8},{0,12},{5,1},{9,5},{13,9},{1,13},{6,2},{10,6},{... | collective-permute-start | bytes 958472 | tf_op jit(solution)/shard_map/ppermute | solution.py:142
  53.7 7.3 %divide_add_fusion.5 = f32[13,17,8,128]{3,1,2,0:T(8,128)S(1)} fusion(f32[13,22,8,128]{3,1,2,0:T(8,128)S(1)} %broadcast_select_fusion.2, f32[13,22,8,128]{3,1,2,0:T(8,128)S(1)} %pad_maximum_fusion.15, f32[17,8,128]{2,0,1:T(8,128)S(1)} %fusion.156), kind=kLoop, calls=%fused_computation.201 | loop fusion | flops 32361472 | bytes 11837440 | tf_op jit(solution)/shard_map/add | solution.py:239
  69.1 9.2 %divide_add_fusion.2 = f32[13,16,8,129]{3,1,2,0:T(8,128)S(1)} fusion(f32[13,16,14,131]{3,1,2,0:T(8,128)S(1)} %get-tuple-element.329, f32[13,16,8,134]{3,1,2,0:T(8,128)S(1)} %pad_maximum_fusion.6, f32[13,16,14,131]{3,1,2,0:T(8,128)S(1)} %get-tuple-element.328, f32[16,8,129]{2,0,1:T(8,128)S(1)} %fusion.117), kind=kLoop, calls=%fused_computation.132 | loop fusion | flops 30695808 | bytes 11228160 | tf_op jit(solution)/shard_map/add | solution.py:239
  78.4 5.4 %divide_add_fusion.8 = f32[13,16,9,128]{3,1,2,0:T(8,128)S(1)} fusion(f32[13,16,3,128]{3,1,2,0:T(8,128)S(1)} %collective-permute-done.4, f32[13,16,8,128]{3,1,2,0:T(8,128)S(1)} %fusion.79, f32[13,16,14,128]{3,1,2,0:T(8,128)S(1)} %pad_maximum_fusion.10, f32[13,16,3,128]{3,1,2,0:T(8,128)S(1)} %collective-permute-done.3, f32[16,9,128]{2,0,1:T(8,128)S(1)} %fusion.171), kind=kLoop, calls=%fused_computation.297 | loop fusion | flops 35702784 | bytes 8273920 | tf_op jit(solution)/shard_map/add | solution.py:239
  90.1 4.6 %collective-permute-start.12 = (f32[13,16,8,3]{1,2,3,0:T(8,128)}, f32[13,16,8,3]{1,2,3,0:T(8,128)}, u32[]{:S(2)}, u32[]{:S(2)}) collective-permute-start(f32[13,16,8,3]{1,2,3,0:T(8,128)} %copy.277), channel_id=1, source_target_pairs={{1,0},{2,1},{3,2},{0,3},{5,4},{6,5},{7,6},{4,7},{9,8},{10,9},{11,1... | collective-permute-start | bytes 59912 | tf_op jit(solution)/shard_map/ppermute | solution.py:142
  104.4 5.5 %collective-permute-start.9 = (f32[13,16,3,128]{3,1,2,0:T(8,128)}, f32[13,16,3,128]{3,1,2,0:T(8,128)S(1)}, u32[]{:S(2)}, u32[]{:S(2)}) collective-permute-start(f32[13,16,3,128]{3,1,2,0:T(8,128)} %get-tuple-element.351), channel_id=1, source_target_pairs={{0,4},{4,8},{8,12},{12,0},{1,5},{5,9},{9,13},{13,1},{2,6},{6,10},{... | collective-permute-start | bytes 958472 | tf_op jit(solution)/shard_map/ppermute | solution.py:141
  117.1 7.1 %divide_add_fusion.4 = f32[13,17,8,128]{3,1,2,0:T(8,128)S(1)} fusion(f32[13,22,8,128]{3,1,2,0:T(8,128)S(1)} %broadcast_select_fusion.1, f32[13,22,8,128]{3,1,2,0:T(8,128)S(1)} %pad_maximum_fusion.16, f32[17,8,128]{2,0,1:T(8,128)S(1)} %fusion.152), kind=kLoop, calls=%fused_computation.194 | loop fusion | flops 32361472 | bytes 11837440 | tf_op jit(solution)/shard_map/add | solution.py:239
  133.4 9.2 %divide_add_fusion.1 = f32[13,16,8,129]{3,1,2,0:T(8,128)S(1)} fusion(f32[13,16,14,131]{3,1,2,0:T(8,128)S(1)} %get-tuple-element.326, f32[13,16,8,134]{3,1,2,0:T(8,128)S(1)} %pad_maximum_fusion.7, f32[13,16,14,131]{3,1,2,0:T(8,128)S(1)} %get-tuple-element.325, f32[16,8,129]{2,0,1:T(8,128)S(1)} %fusion.113), kind=kLoop, calls=%fused_computation.125 | loop fusion | flops 30695808 | bytes 11228160 | tf_op jit(solution)/shard_map/add | solution.py:239
  142.8 5.4 %divide_add_fusion.7 = f32[13,16,9,128]{3,1,2,0:T(8,128)S(1)} fusion(f32[13,16,3,128]{3,1,2,0:T(8,128)S(1)} %collective-permute-done.10, f32[13,16,8,128]{3,1,2,0:T(8,128)S(1)} %fusion.97, f32[13,16,14,128]{3,1,2,0:T(8,128)S(1)} %pad_maximum_fusion.12, f32[13,16,3,128]{3,1,2,0:T(8,128)S(1)} %collective-permute-done.9, f32[16,9,128]{2,0,1:T(8,128)S(1)} %fusion.170), kind=kLoop, calls=%fused_computation.290 | loop fusion | flops 35702784 | bytes 8273920 | tf_op jit(solution)/shard_map/add | solution.py:239
  154.5 4.6 %collective-permute-start.18 = (f32[13,16,8,3]{1,2,3,0:T(8,128)}, f32[13,16,8,3]{1,2,3,0:T(8,128)}, u32[]{:S(2)}, u32[]{:S(2)}) collective-permute-start(f32[13,16,8,3]{1,2,3,0:T(8,128)} %copy.281), channel_id=1, source_target_pairs={{1,0},{2,1},{3,2},{0,3},{5,4},{6,5},{7,6},{4,7},{9,8},{10,9},{11,1... | collective-permute-start | bytes 59912 | tf_op jit(solution)/shard_map/ppermute | solution.py:142
  168.2 5.1 %collective-permute-start.15 = (f32[13,16,3,128]{3,1,2,0:T(8,128)}, f32[13,16,3,128]{3,1,2,0:T(8,128)}, u32[]{:S(2)}, u32[]{:S(2)}) collective-permute-start(f32[13,16,3,128]{3,1,2,0:T(8,128)} %get-tuple-element.345), channel_id=1, source_target_pairs={{0,4},{4,8},{8,12},{12,0},{1,5},{5,9},{9,13},{13,1},{2,6},{6,10},{... | collective-permute-start | bytes 958472 | tf_op jit(solution)/shard_map/ppermute | solution.py:141
  182.8 7.1 %divide_add_fusion.3 = f32[13,17,8,128]{3,1,2,0:T(8,128)S(1)} fusion(f32[13,22,8,128]{3,1,2,0:T(8,128)S(1)} %broadcast_select_fusion, f32[13,22,8,128]{3,1,2,0:T(8,128)S(1)} %pad_maximum_fusion.17, f32[17,8,128]{2,0,1:T(8,128)S(1)} %fusion.148), kind=kLoop, calls=%fused_computation.187 | loop fusion | flops 32361472 | bytes 11837440 | tf_op jit(solution)/shard_map/add | solution.py:239
  202.0 9.2 %divide_add_fusion = f32[13,16,8,129]{3,1,2,0:T(8,128)S(1)} fusion(f32[13,16,14,131]{3,1,2,0:T(8,128)S(1)} %get-tuple-element.323, f32[13,16,8,134]{3,1,2,0:T(8,128)S(1)} %pad_maximum_fusion.8, f32[13,16,14,131]{3,1,2,0:T(8,128)S(1)} %get-tuple-element.322, f32[16,8,129]{2,0,1:T(8,128)S(1)} %fusion.109), kind=kLoop, calls=%fused_computation.118 | loop fusion | flops 30695808 | bytes 11228160 | tf_op jit(solution)/shard_map/add | solution.py:239
  211.3 5.9 %divide_add_fusion.6 = f32[13,16,9,128]{3,1,2,0:T(8,128)S(1)} fusion(f32[13,16,3,128]{3,1,2,0:T(8,128)S(1)} %collective-permute-done.16, f32[13,16,8,128]{3,1,2,0:T(8,128)S(1)} %fusion.92, f32[13,16,14,128]{3,1,2,0:T(8,128)S(1)} %pad_maximum_fusion.14, f32[13,16,3,128]{3,1,2,0:T(8,128)} %collective-permute-done.15, f32[16,9,128]{2,0,1:T(8,128)S(1)} %fusion.169), kind=kLoop, calls=%fused_computation.283 | loop fusion | flops 35702784 | bytes 8273920 | tf_op jit(solution)/shard_map/add | solution.py:239
  220.2 219.6 %while.25 = (s32[]{:T(128)}, f32[16,9,1024]{2,1,0:T(8,128)S(1)}, s32[16]{0:T(128)S(1)}, f32[9,16384]{1,0:T(8,128)S(1)}, s32[16384]{0:T(1024)}, /*index=5*/f32[16...) while((s32[]{:T(128)}, f32[16,9,1024]{2,1,0:T(8,128)S(1)}, ...), condition=%wide.region_53.54_spmd.clone, body=%wide.region_47.53_spmd.sunk.clone.sunk | while | flops 546823 | bytes 880584 | solution.py:293
  223.0 10.9 %while.26 = (s32[]{:T(128)}, f32[9,1024]{1,0:T(8,128)S(1)}, s32[]{:T(128)}, s32[1024]{0:T(1024)S(1)}, f32[1024]{0:T(1024)S(1)}, /*index=5*/f32[1024]{0:T(1024)S(...) while((s32[]{:T(128)}, f32[9,1024]{1,0:T(8,128)S(1)}, ...), condition=%wide.region_52.52_spmd.clone, body=%wide.region_49.51_spmd.sunk.clone.sunk | while | flops 543746 | bytes 650361 | solution.py:279
  236.7 10.9 %while.26 = (s32[]{:T(128)}, f32[9,1024]{1,0:T(8,128)S(1)}, s32[]{:T(128)}, s32[1024]{0:T(1024)S(1)}, f32[1024]{0:T(1024)S(1)}, /*index=5*/f32[1024]{0:T(1024)S(...) while((s32[]{:T(128)}, f32[9,1024]{1,0:T(8,128)S(1)}, ...), condition=%wide.region_52.52_spmd.clone, body=%wide.region_49.51_spmd.sunk.clone.sunk | while | flops 543746 | bytes 650361 | solution.py:279
  250.4 10.9 %while.26 = (s32[]{:T(128)}, f32[9,1024]{1,0:T(8,128)S(1)}, s32[]{:T(128)}, s32[1024]{0:T(1024)S(1)}, f32[1024]{0:T(1024)S(1)}, /*index=5*/f32[1024]{0:T(1024)S(...) while((s32[]{:T(128)}, f32[9,1024]{1,0:T(8,128)S(1)}, ...), condition=%wide.region_52.52_spmd.clone, body=%wide.region_49.51_spmd.sunk.clone.sunk | while | flops 543746 | bytes 650361 | solution.py:279
  264.2 10.9 %while.26 = (s32[]{:T(128)}, f32[9,1024]{1,0:T(8,128)S(1)}, s32[]{:T(128)}, s32[1024]{0:T(1024)S(1)}, f32[1024]{0:T(1024)S(1)}, /*index=5*/f32[1024]{0:T(1024)S(...) while((s32[]{:T(128)}, f32[9,1024]{1,0:T(8,128)S(1)}, ...), condition=%wide.region_52.52_spmd.clone, body=%wide.region_49.51_spmd.sunk.clone.sunk | while | flops 543746 | bytes 650361 | solution.py:279
  277.9 10.9 %while.26 = (s32[]{:T(128)}, f32[9,1024]{1,0:T(8,128)S(1)}, s32[]{:T(128)}, s32[1024]{0:T(1024)S(1)}, f32[1024]{0:T(1024)S(1)}, /*index=5*/f32[1024]{0:T(1024)S(...) while((s32[]{:T(128)}, f32[9,1024]{1,0:T(8,128)S(1)}, ...), condition=%wide.region_52.52_spmd.clone, body=%wide.region_49.51_spmd.sunk.clone.sunk | while | flops 543746 | bytes 650361 | solution.py:279
  291.6 10.9 %while.26 = (s32[]{:T(128)}, f32[9,1024]{1,0:T(8,128)S(1)}, s32[]{:T(128)}, s32[1024]{0:T(1024)S(1)}, f32[1024]{0:T(1024)S(1)}, /*index=5*/f32[1024]{0:T(1024)S(...) while((s32[]{:T(128)}, f32[9,1024]{1,0:T(8,128)S(1)}, ...), condition=%wide.region_52.52_spmd.clone, body=%wide.region_49.51_spmd.sunk.clone.sunk | while | flops 543746 | bytes 650361 | solution.py:279
  305.4 10.9 %while.26 = (s32[]{:T(128)}, f32[9,1024]{1,0:T(8,128)S(1)}, s32[]{:T(128)}, s32[1024]{0:T(1024)S(1)}, f32[1024]{0:T(1024)S(1)}, /*index=5*/f32[1024]{0:T(1024)S(...) while((s32[]{:T(128)}, f32[9,1024]{1,0:T(8,128)S(1)}, ...), condition=%wide.region_52.52_spmd.clone, body=%wide.region_49.51_spmd.sunk.clone.sunk | while | flops 543746 | bytes 650361 | solution.py:279
  319.1 10.9 %while.26 = (s32[]{:T(128)}, f32[9,1024]{1,0:T(8,128)S(1)}, s32[]{:T(128)}, s32[1024]{0:T(1024)S(1)}, f32[1024]{0:T(1024)S(1)}, /*index=5*/f32[1024]{0:T(1024)S(...) while((s32[]{:T(128)}, f32[9,1024]{1,0:T(8,128)S(1)}, ...), condition=%wide.region_52.52_spmd.clone, body=%wide.region_49.51_spmd.sunk.clone.sunk | while | flops 543746 | bytes 650361 | solution.py:279
  332.8 10.9 %while.26 = (s32[]{:T(128)}, f32[9,1024]{1,0:T(8,128)S(1)}, s32[]{:T(128)}, s32[1024]{0:T(1024)S(1)}, f32[1024]{0:T(1024)S(1)}, /*index=5*/f32[1024]{0:T(1024)S(...) while((s32[]{:T(128)}, f32[9,1024]{1,0:T(8,128)S(1)}, ...), condition=%wide.region_52.52_spmd.clone, body=%wide.region_49.51_spmd.sunk.clone.sunk | while | flops 543746 | bytes 650361 | solution.py:279
  346.5 10.9 %while.26 = (s32[]{:T(128)}, f32[9,1024]{1,0:T(8,128)S(1)}, s32[]{:T(128)}, s32[1024]{0:T(1024)S(1)}, f32[1024]{0:T(1024)S(1)}, /*index=5*/f32[1024]{0:T(1024)S(...) while((s32[]{:T(128)}, f32[9,1024]{1,0:T(8,128)S(1)}, ...), condition=%wide.region_52.52_spmd.clone, body=%wide.region_49.51_spmd.sunk.clone.sunk | while | flops 543746 | bytes 650361 | solution.py:279
  360.3 10.9 %while.26 = (s32[]{:T(128)}, f32[9,1024]{1,0:T(8,128)S(1)}, s32[]{:T(128)}, s32[1024]{0:T(1024)S(1)}, f32[1024]{0:T(1024)S(1)}, /*index=5*/f32[1024]{0:T(1024)S(...) while((s32[]{:T(128)}, f32[9,1024]{1,0:T(8,128)S(1)}, ...), condition=%wide.region_52.52_spmd.clone, body=%wide.region_49.51_spmd.sunk.clone.sunk | while | flops 543746 | bytes 650361 | solution.py:279
  374.0 10.9 %while.26 = (s32[]{:T(128)}, f32[9,1024]{1,0:T(8,128)S(1)}, s32[]{:T(128)}, s32[1024]{0:T(1024)S(1)}, f32[1024]{0:T(1024)S(1)}, /*index=5*/f32[1024]{0:T(1024)S(...) while((s32[]{:T(128)}, f32[9,1024]{1,0:T(8,128)S(1)}, ...), condition=%wide.region_52.52_spmd.clone, body=%wide.region_49.51_spmd.sunk.clone.sunk | while | flops 543746 | bytes 650361 | solution.py:279
  387.7 10.9 %while.26 = (s32[]{:T(128)}, f32[9,1024]{1,0:T(8,128)S(1)}, s32[]{:T(128)}, s32[1024]{0:T(1024)S(1)}, f32[1024]{0:T(1024)S(1)}, /*index=5*/f32[1024]{0:T(1024)S(...) while((s32[]{:T(128)}, f32[9,1024]{1,0:T(8,128)S(1)}, ...), condition=%wide.region_52.52_spmd.clone, body=%wide.region_49.51_spmd.sunk.clone.sunk | while | flops 543746 | bytes 650361 | solution.py:279
  401.4 10.9 %while.26 = (s32[]{:T(128)}, f32[9,1024]{1,0:T(8,128)S(1)}, s32[]{:T(128)}, s32[1024]{0:T(1024)S(1)}, f32[1024]{0:T(1024)S(1)}, /*index=5*/f32[1024]{0:T(1024)S(...) while((s32[]{:T(128)}, f32[9,1024]{1,0:T(8,128)S(1)}, ...), condition=%wide.region_52.52_spmd.clone, body=%wide.region_49.51_spmd.sunk.clone.sunk | while | flops 543746 | bytes 650361 | solution.py:279
  415.2 10.9 %while.26 = (s32[]{:T(128)}, f32[9,1024]{1,0:T(8,128)S(1)}, s32[]{:T(128)}, s32[1024]{0:T(1024)S(1)}, f32[1024]{0:T(1024)S(1)}, /*index=5*/f32[1024]{0:T(1024)S(...) while((s32[]{:T(128)}, f32[9,1024]{1,0:T(8,128)S(1)}, ...), condition=%wide.region_52.52_spmd.clone, body=%wide.region_49.51_spmd.sunk.clone.sunk | while | flops 543746 | bytes 650361 | solution.py:279
  428.9 10.9 %while.26 = (s32[]{:T(128)}, f32[9,1024]{1,0:T(8,128)S(1)}, s32[]{:T(128)}, s32[1024]{0:T(1024)S(1)}, f32[1024]{0:T(1024)S(1)}, /*index=5*/f32[1024]{0:T(1024)S(...) while((s32[]{:T(128)}, f32[9,1024]{1,0:T(8,128)S(1)}, ...), condition=%wide.region_52.52_spmd.clone, body=%wide.region_49.51_spmd.sunk.clone.sunk | while | flops 543746 | bytes 650361 | solution.py:279
  (1633 shorter events, 212.0 us)
Async XLA Ops:
  0.0 3.3 copy-start.8
  1.2 18.2 %copy-start.10 = (f32[13,8,128]{2,1,0:T(8,128)S(1)}, f32[13,8,128]{2,1,0:T(8,128)}, u32[]{:S(2)}) copy-start(f32[13,8,128]{2,1,0:T(8,128)} %param.40) | copy-start | bytes 159748
  1.2 18.1 %collective-permute-start = (f32[13,12,8,128]{3,2,1,0:T(8,128)S(1)}, f32[13,12,8,128]{3,2,1,0:T(8,128)S(1)}, u32[]{:S(2)}, u32[]{:S(2)}) collective-permute-start(f32[13,12,8,128]{3,2,1,0:T(8,128)S(1)} %slice.1039), channel_id=1, source_target_pairs={{16,0},{32,16},{48,32},{64,48},{80,64},{96,80},{112,96},{128,112},... | collective-permute-start | bytes 1916936 | tf_op jit(solution)/shard_map/ppermute | solution.py:113
  21.6 19.5 %collective-permute-start.5 = (f32[13,16,8,3]{1,2,3,0:T(8,128)S(1)}, f32[13,16,8,3]{1,2,3,0:T(8,128)S(1)}, u32[]{:S(2)}, u32[]{:S(2)}) collective-permute-start(f32[13,16,8,3]{1,2,3,0:T(8,128)S(1)} %copy.271), channel_id=1, source_target_pairs={{0,1},{1,2},{2,3},{3,0},{4,5},{5,6},{6,7},{7,4},{8,9},{9,10},{10,1... | collective-permute-start | bytes 59912 | tf_op jit(solution)/shard_map/ppermute | solution.py:141
  26.1 21.7 %collective-permute-start.6 = (f32[13,16,8,3]{1,2,3,0:T(8,128)}, f32[13,16,8,3]{1,2,3,0:T(8,128)}, u32[]{:S(2)}, u32[]{:S(2)}) collective-permute-start(f32[13,16,8,3]{1,2,3,0:T(8,128)} %copy.273), channel_id=1, source_target_pairs={{1,0},{2,1},{3,2},{0,3},{5,4},{6,5},{7,6},{4,7},{9,8},{10,9},{11,1... | collective-permute-start | bytes 59912 | tf_op jit(solution)/shard_map/ppermute | solution.py:142
  29.5 22.2 %collective-permute-start.2 = (f32[13,3,8,128]{3,1,2,0:T(4,128)}, f32[13,3,8,128]{3,1,2,0:T(4,128)S(1)}, u32[]{:S(2)}, u32[]{:S(2)}) collective-permute-start(f32[13,3,8,128]{3,1,2,0:T(4,128)} %get-tuple-element.354), channel_id=1, source_target_pairs={{16,0},{32,16},{48,32},{64,48},{80,64},{96,80},{112,96},{128,112},... | collective-permute-start | bytes 479240 | tf_op jit(solution)/shard_map/ppermute | solution.py:126
  31.4 20.2 %collective-permute-start.1 = (f32[13,3,8,128]{3,1,2,0:T(4,128)}, f32[13,3,8,128]{3,1,2,0:T(4,128)S(1)}, u32[]{:S(2)}, u32[]{:S(2)}) collective-permute-start(f32[13,3,8,128]{3,1,2,0:T(4,128)} %get-tuple-element.353), channel_id=1, source_target_pairs={{0,16},{16,32},{32,48},{48,64},{64,80},{80,96},{96,112},{112,128},... | collective-permute-start | bytes 479240 | tf_op jit(solution)/shard_map/ppermute | solution.py:124
  36.6 24.4 %collective-permute-start.4 = (f32[13,16,3,128]{3,1,2,0:T(8,128)}, f32[13,16,3,128]{3,1,2,0:T(8,128)S(1)}, u32[]{:S(2)}, u32[]{:S(2)}) collective-permute-start(f32[13,16,3,128]{3,1,2,0:T(8,128)} %get-tuple-element.358), channel_id=1, source_target_pairs={{4,0},{8,4},{12,8},{0,12},{5,1},{9,5},{13,9},{1,13},{6,2},{10,6},{... | collective-permute-start | bytes 958472 | tf_op jit(solution)/shard_map/ppermute | solution.py:142
  41.1 19.9 %collective-permute-start.3 = (f32[13,16,3,128]{3,1,2,0:T(8,128)}, f32[13,16,3,128]{3,1,2,0:T(8,128)S(1)}, u32[]{:S(2)}, u32[]{:S(2)}) collective-permute-start(f32[13,16,3,128]{3,1,2,0:T(8,128)} %get-tuple-element.357), channel_id=1, source_target_pairs={{0,4},{4,8},{8,12},{12,0},{1,5},{5,9},{9,13},{13,1},{2,6},{6,10},{... | collective-permute-start | bytes 958472 | tf_op jit(solution)/shard_map/ppermute | solution.py:141
  65.5 1.9 slice-start
  69.1 9.2 %slice-start.3 = ((f32[13,16,14,128]{3,1,2,0:T(8,128)}), f32[10,16,14,128]{3,1,2,0:T(8,128)S(1)}, s32[]{:S(2)}) async-start(f32[13,16,14,128]{3,1,2,0:T(8,128)} %copy-done.4), calls=%async_computation.3 | async-start | bytes 2293760 | tf_op jit(solution)/shard_map/slice | solution.py:216
  86.9 16.9 %collective-permute-start.11 = (f32[13,16,8,3]{1,2,3,0:T(8,128)}, f32[13,16,8,3]{1,2,3,0:T(8,128)S(1)}, u32[]{:S(2)}, u32[]{:S(2)}) collective-permute-start(f32[13,16,8,3]{1,2,3,0:T(8,128)} %copy.275), channel_id=1, source_target_pairs={{0,1},{1,2},{2,3},{3,0},{4,5},{5,6},{6,7},{7,4},{8,9},{9,10},{10,1... | collective-permute-start | bytes 59912 | tf_op jit(solution)/shard_map/ppermute | solution.py:141
  90.1 22.7 %collective-permute-start.12 = (f32[13,16,8,3]{1,2,3,0:T(8,128)}, f32[13,16,8,3]{1,2,3,0:T(8,128)}, u32[]{:S(2)}, u32[]{:S(2)}) collective-permute-start(f32[13,16,8,3]{1,2,3,0:T(8,128)} %copy.277), channel_id=1, source_target_pairs={{1,0},{2,1},{3,2},{0,3},{5,4},{6,5},{7,6},{4,7},{9,8},{10,9},{11,1... | collective-permute-start | bytes 59912 | tf_op jit(solution)/shard_map/ppermute | solution.py:142
  94.7 19.9 %collective-permute-start.8 = (f32[13,3,8,128]{3,1,2,0:T(4,128)}, f32[13,3,8,128]{3,1,2,0:T(4,128)S(1)}, u32[]{:S(2)}, u32[]{:S(2)}) collective-permute-start(f32[13,3,8,128]{3,1,2,0:T(4,128)} %get-tuple-element.348), channel_id=1, source_target_pairs={{16,0},{32,16},{48,32},{64,48},{80,64},{96,80},{112,96},{128,112},... | collective-permute-start | bytes 479240 | tf_op jit(solution)/shard_map/ppermute | solution.py:126
  96.6 18.0 %collective-permute-start.7 = (f32[13,3,8,128]{3,1,2,0:T(4,128)}, f32[13,3,8,128]{3,1,2,0:T(4,128)}, u32[]{:S(2)}, u32[]{:S(2)}) collective-permute-start(f32[13,3,8,128]{3,1,2,0:T(4,128)} %get-tuple-element.347), channel_id=1, source_target_pairs={{0,16},{16,32},{32,48},{48,64},{64,80},{80,96},{96,112},{112,128},... | collective-permute-start | bytes 479240 | tf_op jit(solution)/shard_map/ppermute | solution.py:124
  101.8 22.5 %collective-permute-start.10 = (f32[13,16,3,128]{3,1,2,0:T(8,128)}, f32[13,16,3,128]{3,1,2,0:T(8,128)S(1)}, u32[]{:S(2)}, u32[]{:S(2)}) collective-permute-start(f32[13,16,3,128]{3,1,2,0:T(8,128)} %get-tuple-element.352), channel_id=1, source_target_pairs={{4,0},{8,4},{12,8},{0,12},{5,1},{9,5},{13,9},{1,13},{6,2},{10,6},{... | collective-permute-start | bytes 958472 | tf_op jit(solution)/shard_map/ppermute | solution.py:142
  104.4 19.9 %collective-permute-start.9 = (f32[13,16,3,128]{3,1,2,0:T(8,128)}, f32[13,16,3,128]{3,1,2,0:T(8,128)S(1)}, u32[]{:S(2)}, u32[]{:S(2)}) collective-permute-start(f32[13,16,3,128]{3,1,2,0:T(8,128)} %get-tuple-element.351), channel_id=1, source_target_pairs={{0,4},{4,8},{8,12},{12,0},{1,5},{5,9},{9,13},{13,1},{2,6},{6,10},{... | collective-permute-start | bytes 958472 | tf_op jit(solution)/shard_map/ppermute | solution.py:141
  124.4 1.4 copy-start
  129.8 1.9 slice-start.1
  133.4 9.2 %slice-start.4 = ((f32[13,16,14,128]{3,1,2,0:T(8,128)}), f32[10,16,14,128]{3,1,2,0:T(8,128)S(1)}, s32[]{:S(2)}) async-start(f32[13,16,14,128]{3,1,2,0:T(8,128)} %copy-done.5), calls=%async_computation.4 | async-start | bytes 2293760 | tf_op jit(solution)/shard_map/slice | solution.py:216
  151.2 17.0 %collective-permute-start.17 = (f32[13,16,8,3]{1,2,3,0:T(8,128)}, f32[13,16,8,3]{1,2,3,0:T(8,128)S(1)}, u32[]{:S(2)}, u32[]{:S(2)}) collective-permute-start(f32[13,16,8,3]{1,2,3,0:T(8,128)} %copy.279), channel_id=1, source_target_pairs={{0,1},{1,2},{2,3},{3,0},{4,5},{5,6},{6,7},{7,4},{8,9},{9,10},{10,1... | collective-permute-start | bytes 59912 | tf_op jit(solution)/shard_map/ppermute | solution.py:141
  154.5 21.8 %collective-permute-start.18 = (f32[13,16,8,3]{1,2,3,0:T(8,128)}, f32[13,16,8,3]{1,2,3,0:T(8,128)}, u32[]{:S(2)}, u32[]{:S(2)}) collective-permute-start(f32[13,16,8,3]{1,2,3,0:T(8,128)} %copy.281), channel_id=1, source_target_pairs={{1,0},{2,1},{3,2},{0,3},{5,4},{6,5},{7,6},{4,7},{9,8},{10,9},{11,1... | collective-permute-start | bytes 59912 | tf_op jit(solution)/shard_map/ppermute | solution.py:142
  159.1 21.0 %collective-permute-start.14 = (f32[13,3,8,128]{3,1,2,0:T(4,128)}, f32[13,3,8,128]{3,1,2,0:T(4,128)}, u32[]{:S(2)}, u32[]{:S(2)}) collective-permute-start(f32[13,3,8,128]{3,1,2,0:T(4,128)} %get-tuple-element.342), channel_id=1, source_target_pairs={{16,0},{32,16},{48,32},{64,48},{80,64},{96,80},{112,96},{128,112},... | collective-permute-start | bytes 479240 | tf_op jit(solution)/shard_map/ppermute | solution.py:126
  161.0 19.1 %collective-permute-start.13 = (f32[13,3,8,128]{3,1,2,0:T(4,128)}, f32[13,3,8,128]{3,1,2,0:T(4,128)}, u32[]{:S(2)}, u32[]{:S(2)}) collective-permute-start(f32[13,3,8,128]{3,1,2,0:T(4,128)} %get-tuple-element.341), channel_id=1, source_target_pairs={{0,16},{16,32},{32,48},{48,64},{64,80},{80,96},{96,112},{112,128},... | collective-permute-start | bytes 479240 | tf_op jit(solution)/shard_map/ppermute | solution.py:124
  166.1 23.8 %collective-permute-start.16 = (f32[13,16,3,128]{3,1,2,0:T(8,128)}, f32[13,16,3,128]{3,1,2,0:T(8,128)S(1)}, u32[]{:S(2)}, u32[]{:S(2)}) collective-permute-start(f32[13,16,3,128]{3,1,2,0:T(8,128)} %get-tuple-element.346), channel_id=1, source_target_pairs={{4,0},{8,4},{12,8},{0,12},{5,1},{9,5},{13,9},{1,13},{6,2},{10,6},{... | collective-permute-start | bytes 958472 | tf_op jit(solution)/shard_map/ppermute | solution.py:142
  168.2 21.7 %collective-permute-start.15 = (f32[13,16,3,128]{3,1,2,0:T(8,128)}, f32[13,16,3,128]{3,1,2,0:T(8,128)}, u32[]{:S(2)}, u32[]{:S(2)}) collective-permute-start(f32[13,16,3,128]{3,1,2,0:T(8,128)} %get-tuple-element.345), channel_id=1, source_target_pairs={{0,4},{4,8},{8,12},{12,0},{1,5},{5,9},{9,13},{13,1},{2,6},{6,10},{... | collective-permute-start | bytes 958472 | tf_op jit(solution)/shard_map/ppermute | solution.py:141
  178.8 1.3 copy-start.11
  197.4 1.9 slice-start.2
  202.0 9.2 %slice-start.5 = ((f32[13,16,14,128]{3,1,2,0:T(8,128)}), f32[10,16,14,128]{3,1,2,0:T(8,128)S(1)}, s32[]{:S(2)}) async-start(f32[13,16,14,128]{3,1,2,0:T(8,128)} %copy-done.6), calls=%async_computation.5 | async-start | bytes 2293760 | tf_op jit(solution)/shard_map/slice | solution.py:216
  218.7 1.3 copy-start.9
  218.7 1.2 copy-start.15
  218.8 1.2 copy-start.16
  (31 other events, 34.1 us)
where the time goes:
time: 448 us; the launch traced here: 441 us
  other arithmetic  182 us (41%)
  loops' own time  121 us (27%)
  starting transfers between devices  63.1 us (14%)
  local copies, waits for them, and re-layouts  57.4 us (13%)
  waiting for transfers between devices  15.1 us (3%)
    another operation x16, loops' own time, react_cells(): return lax.fori_loop(0, turns, advance, constituent_grids)  109 us
    add x9, other arithmetic, flux_change(): weno_side(plus[0], plus[1], plus[2], plus[3], plus[4])  65.9 us
    select_n x128, other arithmetic, advance(): return jnp.where((index < counts)[None], moved, current)  29.3 us
    mul x896, other arithmetic, react_step(): arrhenius_coefficients[constituent_count]  21.8 us
    ppermute x6, starting transfers between devices, padded_2(): lax.ppermute(last, axis, up)  21.4 us
    ppermute x6, starting transfers between devices, padded_2(): lax.ppermute(first, axis, [(b, a) for a, b in up])  21 us
    ppermute x1, waiting for transfers between devices, from_behind(): lax.ppermute(value, axis, [(source, source + steps) for source in range(f...  15.1 us
    ppermute x3, starting transfers between devices, padded(): lax.ppermute(tail, axis, [(i, (i + 1) % count) for i in range(ends)])  12.8 us
  transfers between devices with their start and end apart: 19, of which 1 were waited for; matrix products, arithmetic and copies ran while one was open for 12% of the time, Pallas kernels for 0%

commit v1 on v0

v1 whole, which is shorter than its diff:
```python
import functools

import jax
import jax.numpy as jnp
import numpy as np
from jax import lax
from jax.experimental import pallas as pl
from jax.experimental.pallas import tpu as pltpu
from jax.sharding import PartitionSpec as P

SMAX = 12
CMAX = 8
DT = 0.05
W = [float(w) for w in np.array([2.016, 31.998, 18.015, 1.008, 15.999, 17.007, 33.006, 34.014, 28.014]) / 18.015]
IW = [1.0 / w for w in W]
MESH = pl.DeviceIdType.MESH
F32 = jnp.float32


def total(parts):
    while len(parts) > 1:
        parts = [a + b for a, b in zip(parts[::2], parts[1::2])] + ([parts[-1]] if len(parts) % 2 else [])
    return parts[0]


def gas(u):
    rho = total(list(u[:9]))
    c = [u[k] * IW[k] for k in range(9)]
    s1 = total([c[0], c[1], c[5], c[8]])
    s2 = total([c[2], c[6], c[7]])
    s3 = c[3] + c[4]
    gas_sum = s1 + s2 + s3
    heat = 2.5 * s1 + 3.0 * s2 + 1.5 * s3
    bound = total([-1.5 * u[2], 12.0 * u[3], 1.5 * u[4], 0.25 * u[5], 0.02 * u[6], -0.45 * u[7]])
    r = 1.0 / rho
    kinetic = 0.5 * r * (u[9] * u[9] + u[10] * u[10] + u[11] * u[11])
    over = 1.0 / heat
    pressure = gas_sum * ((u[12] - kinetic - bound) * over)
    sound = jnp.sqrt((1.0 + gas_sum * over) * pressure * r)
    return r, pressure, sound


def one_side(e1, e2, e3, e4):
    k2 = e2 * e2 * 0.609375 + 3e-6
    k3 = e3 * e3 * 0.609375 + 3e-6
    ta = e1 - 1.375 * e2
    tb = e3 - 0.625 * e2
    tc = e4 - 1.375 * e3
    ra = 1.0 / (ta * ta + k2)
    rb = 1.0 / (tb * tb + k2)
    rc = 1.0 / (tc * tc + k3)
    d23 = e3 - e2
    a = ta + tb
    c = d23 - (e4 - e3)
    wa = ra * ra
    wb = rb * rb * 6.0
    wc = rc * rc * 3.0
    return (wc * c - wa * (a + a)) / (wa + wb + wc) - d23


def face(pair_sum, alpha, df, du):
    p = [alpha * d for d in du]
    plus = [df[k] + p[k] for k in range(4)]
    minus = [df[k] - p[k] for k in range(1, 5)]
    x = one_side(plus[0], plus[1], plus[2], plus[3])
    y = one_side(minus[3], minus[2], minus[1], minus[0])
    return 6.0 * pair_sum + (x - y)


def sweep(lo, hi, value, speed, extra, kind, alpha, emit, before=None, after=None):
    us, fs, du, df = {}, {}, {}, {}

    def cell(i):
        u = value(i)
        v = speed(i)
        if kind == 0:
            f = u * v
        elif kind == 1:
            f = u * v + extra(i)
        else:
            f = (u + extra(i)) * v
        us[i], fs[i] = u, f

    def diff(i):
        cell(i + 1)
        du[i] = us[i + 1] - us[i]
        df[i] = fs[i + 1] - fs[i]

    cell(lo - 2)
    for i in range(lo - 2, lo + 2):
        diff(i)
    head = None
    for j in range(lo, hi + 1):
        diff(j + 2)
        now = face(
            fs[j] + fs[j + 1],
            alpha(j),
            [df[j + k] for k in range(-2, 3)],
            [du[j + k] for k in range(-2, 3)],
        )
        head = now if head is None else head
        if before is not None:
            emit(j, now - before)
        before = now
    if after is not None:
        emit(hi + 1, after - before)
    return head, before


def widest(m):
    return jnp.maximum(jnp.maximum(jnp.maximum(m[0], m[1]), jnp.maximum(m[2], m[3])), jnp.maximum(m[4], m[5]))


def step_kernel(
    sizes,
    start, fresh, third,
    first, second, acc, accy, accz, turned, ends,
    xlo, xhi, ylo, yhi, ysl, ysh, zu,
    nat, xt, yt, zt, ax, ay, az,
    send, recv,
):
    n_tube, n_gy, n_gz = sizes
    me_t, me_y, me_z = lax.axis_index("tube"), lax.axis_index("gy"), lax.axis_index("gz")
    has_lo, has_hi = me_t > 0, me_t < n_tube - 1
    y_next, y_prev = lax.rem(me_y + 1, n_gy), lax.rem(me_y + n_gy - 1, n_gy)
    z_next, z_prev = lax.rem(me_z + 1, n_gz), lax.rem(me_z + n_gz - 1, n_gz)

    def to(tube=None, gy=None, gz=None):
        return (
            me_t if tube is None else tube,
            me_y if gy is None else gy,
            me_z if gz is None else gz,
        )

    barrier = pltpu.get_barrier_semaphore()
    for there in (to(gy=y_next), to(gy=y_prev), to(gz=z_next), to(gz=z_prev)):
        pl.semaphore_signal(barrier, inc=1, device_id=there, device_id_type=MESH)

    @pl.when(has_lo)
    def _():
        pl.semaphore_signal(barrier, inc=1, device_id=to(tube=me_t - 1), device_id_type=MESH)

    @pl.when(has_hi)
    def _():
        pl.semaphore_signal(barrier, inc=1, device_id=to(tube=me_t + 1), device_id_type=MESH)

    pl.semaphore_wait(barrier, 4 + lax.min(me_t, 1) + lax.min(n_tube - 1 - me_t, 1))

    def remote(src, dst, stage, slot, there):
        return pltpu.make_async_remote_copy(
            src_ref=src, dst_ref=dst, send_sem=send.at[stage, slot], recv_sem=recv.at[stage, slot],
            device_id=there, device_id_type=MESH,
        )

    def copies(stage, cur):
        x_up = remote(cur.at[:, pl.ds(0, 24), :], xhi.at[stage], stage, 0, to(tube=me_t - 1))
        x_down = remote(cur.at[:, pl.ds(104, 24), :], xlo.at[stage], stage, 1, to(tube=me_t + 1))
        y_up = remote(ysh.at[stage], ylo.at[stage], stage, 2, to(gy=y_next))
        y_down = remote(ysl.at[stage], yhi.at[stage], stage, 3, to(gy=y_prev))
        z_up = remote(
            zu.at[stage, :, pl.ds(128, 8), :], zu.at[stage, :, pl.ds(0, 8), :], stage, 4, to(gz=z_next)
        )
        z_down = remote(
            zu.at[stage, :, pl.ds(8, 8), :], zu.at[stage, :, pl.ds(136, 8), :], stage, 5, to(gz=z_prev)
        )
        return x_up, x_down, y_up, y_down, z_up, z_down

    def plane(ref, p):
        return ref[pl.ds(8 * p, 8), :]

    def regular(d, body):
        @pl.loop(0, 11)
        def _(k):
            body(k + (k + 7 - d) // 16, 0)

        body(9 + d, 1)
        body(12, 2)

    def stage_step(stage, cur, out, a, b):
        x_up, x_down, y_up, y_down, z_up, z_down = copies(stage, cur)

        z_up.start()
        z_down.start()

        @pl.when(has_lo)
        def _():
            x_up.start()

        @pl.when(has_hi)
        def _():
            x_down.start()

        @pl.loop(0, 13)
        def _(c):
            for k in range(3):
                for g in range(2):
                    ysl[stage, c, 2 * k + g] = cur[c, pl.ds(64 * g + k, 8, stride=8), :]
                    ysh[stage, c, 2 * k + g] = cur[c, pl.ds(64 * g + 5 + k, 8, stride=8), :]

        y_up.start()
        y_down.start()

        @pl.loop(0, 8)
        def _(q):
            for h in range(2):
                rows = pl.ds(pl.multiple_of(16 * q + 8 * h, 8), 8)
                u = [cur[c, rows, :] for c in range(13)]
                r, pressure, sound = gas(u)
                nat[0, rows, :] = pressure
                for d in range(3):
                    v = u[9 + d] * r
                    nat[1 + d, rows, :] = v
                    nat[4 + d, rows, :] = jnp.abs(v) + sound

        zt[0, pl.ds(8, 128), :] = jnp.transpose(nat[0])
        zt[1, pl.ds(8, 128), :] = jnp.transpose(nat[3])
        zt[2, pl.ds(8, 128), :] = jnp.transpose(nat[6])

        def x_value(c, i):
            if i < 0:
                return xlo[stage, c, pl.ds(8 * (i + 3), 8), :]
            if i > 15:
                return xhi[stage, c, pl.ds(8 * (i - 16), 8), :]
            return cur[c, pl.ds(8 * i, 8), :]

        def x_of(row, nat_row, i):
            if i < 0:
                return xt[row, i + 3]
            if i > 15:
                return xt[row, i - 13]
            return nat[nat_row, pl.ds(8 * i, 8), :]

        def x_alpha(j):
            ax[j + 1] = widest([x_of(2, 4, j + k) for k in range(-2, 4)])

        def x_sweep(c, kind, lo, hi, **known):
            def emit(i, change):
                rows = pl.ds(8 * i, 8)
                acc[c, rows, :] = change

            return sweep(
                lo, hi, lambda i: x_value(c, i), lambda i: x_of(1, 1, i), lambda i: x_of(0, 0, i),
                kind, lambda j: ax[j + 1], emit, **known,
            )

        for j in range(2, 13):
            x_alpha(j)

        def x_inner(c, kind):
            ends[c, 0], ends[c, 1] = x_sweep(c, kind, 2, 12)

        regular(0, x_inner)

        z_up.wait_recv()
        z_down.wait_recv()
        for h in range(2):
            rows = pl.ds(136 * h, 8)
            r, pressure, sound = gas([zu[stage, c, rows, :] for c in range(13)])
            v = zu[stage, 11, rows, :] * r
            zt[0, rows, :] = pressure
            zt[1, rows, :] = v
            zt[2, rows, :] = jnp.abs(v) + sound

        def z_rows(i):
            return pl.ds(8 + i, 8, stride=16)

        for j in range(-1, 16):
            az[j + 1] = widest([zt[2, z_rows(j + k), :] for k in range(-2, 4)])

        def z_body(c, kind):
            def emit(i, change):
                accz[c, pl.ds(i, 8, stride=16), :] = change

            sweep(
                -1, 15, lambda i: zu[stage, c, z_rows(i), :], lambda i: zt[1, z_rows(i), :],
                lambda i: zt[0, z_rows(i), :], kind, lambda j: az[j + 1], emit,
            )

        regular(2, z_body)

        @pl.when(has_lo)
        def _():
            x_down.wait_recv()

        @pl.when(has_hi)
        def _():
            x_up.wait_recv()

        @pl.when(jnp.logical_not(has_lo))
        def _():
            @pl.loop(0, 13)
            def _(c):
                for k in range(3):
                    xlo[stage, c, pl.ds(8 * k, 8), :] = cur[c, pl.ds(0, 8), :]

        @pl.when(jnp.logical_not(has_hi))
        def _():
            @pl.loop(0, 13)
            def _(c):
                for k in range(3):
                    xhi[stage, c, pl.ds(8 * k, 8), :] = fresh[c]

        for i in (-3, -2, -1, 16, 17, 18):
            u = [x_value(c, i) for c in range(13)]
            r, pressure, sound = gas(u)
            v = u[9] * r
            k = i + 3 if i < 0 else i - 13
            xt[0, k] = pressure
            xt[1, k] = v
            xt[2, k] = jnp.abs(v) + sound

        for j in (-1, 0, 1, 13, 14, 15):
            x_alpha(j)

        def x_outer(c, kind):
            x_sweep(c, kind, -1, 1, after=ends[c, 0])
            x_sweep(c, kind, 13, 15, before=ends[c, 1])
            turned[c] = jnp.transpose(accz[c])

        regular(0, x_outer)

        y_up.wait_recv()
        y_down.wait_recv()

        def y_value(c, g, i):
            if i < 0:
                return ylo[stage, c, 2 * (i + 3) + g]
            if i > 7:
                return yhi[stage, c, 2 * (i - 8) + g]
            return cur[c, pl.ds(64 * g + i, 8, stride=8), :]

        for g in range(2):
            for i in range(-3, 11):
                k = 2 * (i + 3) + g
                if 0 <= i < 8:
                    for row, nat_row in ((0, 0), (1, 2), (2, 5)):
                        yt[row, k] = nat[nat_row, pl.ds(64 * g + i, 8, stride=8), :]
                else:
                    u = [y_value(c, g, i) for c in range(13)]
                    r, pressure, sound = gas(u)
                    v = u[10] * r
                    yt[0, k] = pressure
                    yt[1, k] = v
                    yt[2, k] = jnp.abs(v) + sound
            for j in range(-1, 8):
                ay[2 * (j + 1) + g] = widest([yt[2, 2 * (j + k + 3) + g] for k in range(-2, 4)])

        def y_body(c, kind):
            for g in range(2):
                def emit(i, change):
                    accy[c, pl.ds(16 * i + 8 * g, 8), :] = change

                sweep(
                    -1, 7, lambda i: y_value(c, g, i), lambda i: yt[1, 2 * (i + 3) + g],
                    lambda i: yt[0, 2 * (i + 3) + g], kind, lambda j: ay[2 * (j + 1) + g], emit,
                )

        regular(1, y_body)

        for c in range(13):
            across = [accy[c, pl.ds(8 * (p // 8) + p % 8, 8, stride=16), :] for p in range(16)]
            change = acc[c] + turned[c] + jnp.concatenate(across, axis=0)
            moved = b * cur[c] - (b * DT / 12.0) * change
            if a != 0.0:
                moved = a * start[c] + moved
            out[c] = moved
            if stage < 2:
                zu[stage + 1, c, pl.ds(8, 128), :] = jnp.transpose(moved)

    for c in range(13):
        zu[0, c, pl.ds(8, 128), :] = jnp.transpose(start[c])
    stage_step(0, start, first, 0.0, 1.0)
    stage_step(1, first, second, 0.75, 0.25)
    stage_step(2, second, third, 1.0 / 3.0, 2.0 / 3.0)

    for stage, cur in enumerate((start, first, second)):
        x_up, x_down, y_up, y_down, z_up, z_down = copies(stage, cur)
        for copy in (y_up, y_down, z_up, z_down):
            copy.wait_send()

        @pl.when(has_lo)
        def _():
            x_up.wait_send()

        @pl.when(has_hi)
        def _():
            x_down.wait_send()


def advance_flow(start, fresh, sizes):
    tile = (8, 128)
    vmem = pl.BlockSpec(memory_space=pltpu.VMEM)
    scratch = [
        pltpu.VMEM((13, 128, 128), F32),
        pltpu.VMEM((13, 128, 128), F32),
        pltpu.VMEM((13, 128, 128), F32),
        pltpu.VMEM((13, 128, 128), F32),
        pltpu.VMEM((13, 128, 128), F32),
        pltpu.VMEM((13, 128, 128), F32),
        pltpu.VMEM((13, 2) + tile, F32),
        pltpu.VMEM((3, 13, 24, 128), F32),
        pltpu.VMEM((3, 13, 24, 128), F32),
        pltpu.VMEM((3, 13, 6) + tile, F32),
        pltpu.VMEM((3, 13, 6) + tile, F32),
        pltpu.VMEM((3, 13, 6) + tile, F32),
        pltpu.VMEM((3, 13, 6) + tile, F32),
        pltpu.VMEM((3, 13, 144, 128), F32),
        pltpu.VMEM((7, 128, 128), F32),
        pltpu.VMEM((3, 6) + tile, F32),
        pltpu.VMEM((3, 28) + tile, F32),
        pltpu.VMEM((3, 144, 128), F32),
        pltpu.VMEM((17,) + tile, F32),
        pltpu.VMEM((18,) + tile, F32),
        pltpu.VMEM((17,) + tile, F32),
        pltpu.SemaphoreType.DMA((3, 6)),
        pltpu.SemaphoreType.DMA((3, 6)),
    ]
    return pl.pallas_call(
        functools.partial(step_kernel, sizes),
        out_shape=jax.ShapeDtypeStruct((13, 128, 128), F32),
        in_specs=[vmem, vmem],
        out_specs=vmem,
        scratch_shapes=scratch,
        compiler_params=pltpu.CompilerParams(collective_id=0, has_side_effects=True),
        name="flow",
    )(start, fresh)


def rates(c, y):
    h = jnp.exp(-0.5 * y)
    g = jnp.exp(-0.3 * y)
    e1 = h * h
    e15 = e1 * h
    e3 = e15 * e15
    e4 = e3 * e1
    e45 = e3 * e15
    e5 = e4 * e1
    e6 = e3 * e3
    e08 = h * g
    c31 = c[3] * c[1]
    c45 = c[4] * c[5]
    c40 = c[4] * c[0]
    c35 = c[3] * c[5]
    n0 = 30.0 * e4 * c31 - 8.0 * e1 * c45
    n2 = 20.0 * e3 * c40 - 6.0 * e15 * c35
    n4 = 25.0 * e15 * (c[0] * c[5]) - 10.0 * e45 * (c[2] * c[3])
    n6 = 12.0 * e4 * (c[4] * c[2]) - 5.0 * e15 * (c[5] * c[5])
    r8 = 4.0 * e6 * (c[0] * c[8])
    third = h * c[8]
    c34 = c[3] * c[4]
    r9 = 20.0 * third * (c[3] * c[3])
    r10 = 15.0 * third * (c[4] * c[4])
    r11 = 18.0 * third * c34
    r12 = 22.0 * third * c35
    r13 = 25.0 * (g * c[8]) * c31
    c63 = c[6] * c[3]
    r14 = 30.0 * e08 * c63
    r15 = 25.0 * h * c63
    r16 = 20.0 * g * (c[6] * c[4])
    r17 = 30.0 * g * (c[6] * c[5])
    r18 = 10.0 * h * (c[6] * c[6])
    r19 = 6.0 * e5 * (c[7] * c[8])
    r20 = 15.0 * e15 * (c[7] * c[3])
    s89 = r8 - r9
    a1113 = r11 + r13
    a1415 = r14 + r15
    a1617 = r16 + r17
    w = [None] * 9
    w[0] = (r14 - n2) - (n4 + s89)
    w[1] = (r10 - n0) + (r14 - r13) + (a1617 + r18)
    w[2] = (n4 - n6) + (r12 + r17) + r20
    w[3] = (n2 - n0) + (n4 + (s89 + s89)) - (a1113 + r12) - (a1415 + r20)
    w[4] = (n0 - n2) - n6 - (r10 + r10) - (r11 + r16)
    two = n6 + r15 + r19
    w[5] = (n0 + n2) - n4 + (two + two) + (r11 - r12) + (r16 - r17) + r20
    w[6] = r13 - (a1415 + a1617) - (r18 + r18)
    w[7] = r18 - (r19 + r20)
    w[8] = -((r8 + r9) + (r10 + r12) + (a1113 + r19))
    return w


def react_kernel(planes, u_ref, n_ref, o_ref):
    def block(q, _):
        rows = [pl.ds(pl.multiple_of(8 * planes * q + 8 * h, 8), 8) for h in range(planes)]
        for row in rows:
            for k in range(9, 13):
                o_ref[k, row, :] = u_ref[k, row, :]
        state = []
        fixed = []
        for row in rows:
            u = [u_ref[k, row, :] for k in range(13)]
            rho = total(u[:9])
            internal = u[12] - 0.5 * (u[9] * u[9] + u[10] * u[10] + u[11] * u[11]) / rho
            counts = n_ref[row, :]
            fixed.append((internal, counts, DT / counts.astype(F32)))
            state.append(tuple(u[k] * IW[k] for k in range(9)))

        def substep(i, state):
            new = []
            for c, (internal, counts, step) in zip(state, fixed):
                s1 = total([c[0], c[1], c[5], c[8]])
                s2 = total([c[2], c[6], c[7]])
                heat = 2.5 * s1 + 3.0 * s2 + 1.5 * (c[3] + c[4])
                bound = total([
                    (-1.5 * W[2]) * c[2], (12.0 * W[3]) * c[3], (1.5 * W[4]) * c[4],
                    (0.25 * W[5]) * c[5], (0.02 * W[6]) * c[6], (-0.45 * W[7]) * c[7],
                ])
                w = rates(c, heat / (internal - bound))
                live = i < counts
                new.append(tuple(jnp.where(live, c[k] + step * w[k], c[k]) for k in range(9)))
            return tuple(new)

        state = lax.fori_loop(0, CMAX, substep, tuple(state))
        for row, c in zip(rows, state):
            for k in range(9):
                o_ref[k, row, :] = c[k] * W[k]
        return 0

    lax.fori_loop(0, u_ref.shape[1] // (8 * planes), block, 0)


def react(third, substeps):
    steps = 4
    size = 128 // steps
    return pl.pallas_call(
        functools.partial(react_kernel, 2),
        out_shape=jax.ShapeDtypeStruct((13, 128, 128), F32),
        grid=(steps,),
        in_specs=[
            pl.BlockSpec((13, size, 128), lambda i: (0, i, 0)),
            pl.BlockSpec((size, 128), lambda i: (i, 0)),
        ],
        out_specs=pl.BlockSpec((13, size, 128), lambda i: (0, i, 0)),
        name="react",
    )(third, substeps)


def on_device(sizes, state, fresh, substeps, shift):
    comps, planes, wy, wz = state.shape
    n_tube = sizes[0]
    ahead = lax.ppermute(state[:, :SMAX], "tube", [(i, i - 1) for i in range(1, n_tube)])
    joined = jnp.concatenate([state, ahead], axis=1)
    start = lax.dynamic_slice_in_dim(joined, shift, planes, 1)
    position = lax.axis_index("tube") * planes + lax.iota(jnp.int32, planes)
    beyond = (position + shift >= n_tube * planes)[None, :, None, None]
    start = jnp.where(beyond, fresh[:, None], start)
    third = advance_flow(start.reshape(comps, planes * wy, wz), fresh, sizes)
    out = react(third, substeps.reshape(planes * wy, wz))
    return out.reshape(comps, planes, wy, wz)


def solution(mesh):
    sizes = tuple(mesh.shape[name] for name in ("tube", "gy", "gz"))
    return jax.shard_map(
        functools.partial(on_device, sizes),
        mesh=mesh,
        in_specs=(P(None, "tube", "gy", "gz"), P(None, "gy", "gz"), P("tube", "gy", "gz"), P()),
        out_specs=P(None, "tube", "gy", "gz"),
        check_vma=False,
    )
```

time: 448 us -> 94.1 us (0.21)
  the two profiles are of different devices: /device:TPU:457 before, /device:TPU:385 now
where the time goes in v1:
time: 94.1 us; the launch traced here: 93.9 us
  Pallas kernels  73.7 us (78%)
  waiting for transfers between devices  12.4 us (13%)
  starting transfers between devices  4.86 us (5%)
  local copies, waits for them, and re-layouts  1.21 us (1%)
  other arithmetic  1.09 us (1%)
    pallas_call x1, Pallas kernels, advance_flow(): pl.pallas_call(functools.partial(step_kernel, sizes), out_shape=jax.Shape...  67.5 us
    ppermute x1, waiting for transfers between devices, on_device(): lax.ppermute(state[:, :SMAX], 'tube', [(i, i - 1) for i in range(1, n_tub...  12.4 us
    pallas_call x1, Pallas kernels, react(): pl.pallas_call(functools.partial(react_kernel, 2), out_shape=jax.ShapeDty...  6.12 us
    ppermute x1, starting transfers between devices, on_device(): lax.ppermute(state[:, :SMAX], 'tube', [(i, i - 1) for i in range(1, n_tub...  4.86 us
  transfers between devices with their start and end apart: 1, of which 1 were waited for; matrix products, arithmetic and copies ran while one was open for 0% of the time, Pallas kernels for 0%

profile of v1, /device:TPU:385, one launch (start us, length us, event | category | flops | bytes accessed | tf_op | source)
XLA Modules:
  0.0 93.9 jit_solution(12159714976937132961)
XLA Ops:
  0.0 0.0 copy-start
  0.0 0.0 copy-start.1
  0.0 1.2 %slice.3 = f32[13,12,8,128]{3,2,1,0:T(8,128)S(1)} slice(f32[13,16,8,128]{3,2,1,0:T(8,128)} %param.4), slice={[0:13], [0:12], [0:8], [0:128]} | slice | bytes 1277952 | tf_op jit(solution)/shard_map/slice | solution.py:541
  1.2 4.9 %collective-permute-start = (f32[13,12,8,128]{3,2,1,0:T(8,128)S(1)}, f32[13,12,8,128]{3,2,1,0:T(8,128)S(1)}, u32[]{:S(2)}, u32[]{:S(2)}) collective-permute-start(f32[13,12,8,128]{3,2,1,0:T(8,128)S(1)} %slice.3), channel_id=1, source_target_pairs={{16,0},{32,16},{48,32},{64,48},{80,64},{96,80},{112,96},{128,112},... | collective-permute-start | bytes 1916936 | tf_op jit(solution)/shard_map/ppermute | solution.py:541
  6.8 12.4 %collective-permute-done = f32[13,12,8,128]{3,2,1,0:T(8,128)S(1)} collective-permute-done((f32[13,12,8,128]{3,2,1,0:T(8,128)S(1)}, f32[13,12,8,128]{3,2,1,0:T(8,128)S(1)}, u32[]{:S(2)}, u32[]{:S(2)}) %collective-permute-start) | collective-permute-done | bytes 639008 | tf_op jit(solution)/shard_map/ppermute | solution.py:541
  19.1 0.0 copy-done
  19.1 0.0 copy-done.1
  19.1 1.1 %fusion.2.start = f32[13,128,128]{2,1,0:T(8,128)} fusion(s32[]{:T(128)S(6)} %select_n.7, f32[13,16,8,128]{3,2,1,0:T(8,128)S(1)} %copy-done, f32[13,12,8,128]{3,2,1,0:T(8,128)S(1)} %collective-permute-done, f32[13,8,128]{2,1,0:T(8,128)S(1)} %copy-done.1, pred[16]{0:T(512)(128)(4,1)S(1)} %add_compare_fusion), kind=kLoop, calls=%fused_computation.4 | loop fusion | flops 425984 | bytes 2396180 | tf_op jit(solution)/shard_map/reshape | solution.py:547
  20.2 67.5 %flow.1.u_ref = f32[13,128,128]{2,1,0:T(8,128)} custom-call(f32[13,128,128]{2,1,0:T(8,128)} %fusion.2.start, f32[13,8,128]{2,1,0:T(8,128)} %fresh.1), custom_call_target="tpu_custom_call" | custom-call | tf_op jit(solution)/shard_map/flow/pallas_call | solution.py:418
  87.8 6.1 %react.1 = f32[13,128,128]{2,1,0:T(8,128)} custom-call(f32[13,128,128]{2,1,0:T(8,128)} %flow.1.u_ref, s32[128,128]{1,0:T(8,128)} %bitcast.4), custom_call_target="tpu_custom_call" | custom-call | tf_op jit(solution)/shard_map/react/pallas_call | solution.py:525
  (1 shorter events, 0.0 us)
Async XLA Ops:
  0.0 19.1 %copy-start = (f32[13,16,8,128]{3,2,1,0:T(8,128)S(1)}, f32[13,16,8,128]{3,2,1,0:T(8,128)}, u32[]{:S(2)}) copy-start(f32[13,16,8,128]{3,2,1,0:T(8,128)} %param.4) | copy-start | bytes 2555908
  0.0 19.1 %copy-start.1 = (f32[13,8,128]{2,1,0:T(8,128)S(1)}, f32[13,8,128]{2,1,0:T(8,128)}, u32[]{:S(2)}) copy-start(f32[13,8,128]{2,1,0:T(8,128)} %fresh.1) | copy-start | bytes 159748
  1.2 17.9 %collective-permute-start = (f32[13,12,8,128]{3,2,1,0:T(8,128)S(1)}, f32[13,12,8,128]{3,2,1,0:T(8,128)S(1)}, u32[]{:S(2)}, u32[]{:S(2)}) collective-permute-start(f32[13,12,8,128]{3,2,1,0:T(8,128)S(1)} %slice.3), channel_id=1, source_target_pairs={{16,0},{32,16},{48,32},{64,48},{80,64},{96,80},{112,96},{128,112},... | collective-permute-start | bytes 1916936 | tf_op jit(solution)/shard_map/ppermute | solution.py:541
